TPU v7x, 32 devices: a whole 2x2x4 slice. The times are simulated.
32 devices in a mesh: grp: 2 (over y), rx: 4 (over z), tw: 2 (over x), fq: 2 (over core).
Axes of the slice: x: 2, y: 2, z: 4, core: 2. Of those that a mesh axis runs over, the one named last changes fastest.
Arguments:
- traces: bfloat16 [8, 256, 15360], P('tw', ('grp', 'rx')), parts along dimension 1, may hold values from -48 to 48
- src_index: int32 [8, 64], P('grp'), parts along dimension 0, may hold values from 0 to 127
- valid: int32 [8, 256], P(None, 'grp'), parts along dimension 1, may hold values from 0 to 1, as said below
Outputs:
- correlations: bfloat16 [256, 256, 512], P(('tw', 'fq'), ('grp', 'rx')), parts along dimension 1
There are 2 independent parts, one for each index of `grp`. A program takes and returns all parts, laid end to end along the dimension named above; each array names one. Nothing has to cross between parts.
Inputs may be any that keep to these rules, and one draw needn't show every extreme that they name: `valid`: some channels may be 0 in every window, and some windows 0 on every channel. `src_index`: A channel may be named by several sources.
All inputs are finite; a program needn't handle non-finite values.
Results may differ from a plain program's by a relative error of at most 0.0062.
Values may be sent and summed in bfloat16 or wider, within the bound.
No kernel may reach another device: no remote copies, remote signals or barrier semaphores. Data moves between devices by JAX's collectives and lax.ppermute only.
A program may use at most 128 MiB of HBM per device.

v0:
```python
import math
import jax
import jax.numpy as jnp
from jax import lax
from jax.sharding import PartitionSpec as P

NT = 15360
BAND = 512
F0 = 60
HW = 32
LAGS = 512
two_pi = 2.0 * math.pi
eps_power = 1e-05


def padded_2(block, sides, width):
    for axis, dim in sides:
        count = lax.axis_size(axis)
        forward = [(i, i + 1) for i in range(count - 1)]
        backward = [(target, source) for source, target in forward]
        low = lax.ppermute(
            lax.slice_in_dim(block, block.shape[dim] - width, None, axis=dim), axis, forward
        )
        high = lax.ppermute(lax.slice_in_dim(block, 0, width, axis=dim), axis, backward)
        block = jnp.concatenate([low, block, high], axis=dim)
    return block


def forward_block(row_count, bin_ids, period):
    sample_ids = lax.broadcasted_iota(jnp.int32, (row_count, 1, 1), 0)
    phase_index = sample_ids * bin_ids[None, :, :] % period
    angle_rad = phase_index.astype(jnp.float32) * (two_pi / period)
    coef_block = jnp.stack([jnp.cos(angle_rad), -jnp.sin(angle_rad)], axis=2)
    return coef_block.reshape(row_count, -1).astype(jnp.bfloat16)


def inverse_rows(bin_ids, lag_count, period):
    lag_shift = lax.broadcasted_iota(jnp.int32, (1, lag_count), 1) - lag_count // 2
    phase_index = bin_ids[..., None] * lag_shift % period
    angle_rad = phase_index.astype(jnp.float32) * (two_pi / period)
    return jnp.concatenate([jnp.cos(angle_rad), -jnp.sin(angle_rad)], axis=-2).astype(jnp.bfloat16)


def shards(traces, src_index, valid):
    win_count, chan_count, samples = traces.shape
    tw_count = lax.axis_size("tw")
    fq_count = lax.axis_size("fq")
    tw_pos = lax.axis_index("tw")
    fq_pos = lax.axis_index("fq")
    rx_pos = lax.axis_index("rx")
    band_share = BAND // fq_count
    narrow = band_share // tw_count
    block_len = 1024
    trace_rows = traces.reshape(win_count * chan_count, samples)
    local_bins = (
        F0
        + fq_pos * band_share
        + lax.broadcasted_iota(jnp.int32, (tw_count, narrow), 0) * narrow
        + lax.broadcasted_iota(jnp.int32, (tw_count, narrow), 1)
    )
    base_table = forward_block(block_len, local_bins, samples)

    def accumulate(turn_index, running):
        offset = turn_index * block_len
        trace_piece = lax.dynamic_slice_in_dim(trace_rows, offset, block_len, 1)
        partial_value = jnp.dot(trace_piece, base_table, preferred_element_type=jnp.float32)
        partial_value = partial_value.reshape(-1, tw_count, 2, narrow)
        part_real = partial_value[:, :, 0]
        part_imag = partial_value[:, :, 1]
        phase_index = offset * local_bins % samples
        angle_rad = phase_index.astype(jnp.float32) * (two_pi / samples)
        turn_real = jnp.cos(angle_rad)[None]
        turn_imag = -jnp.sin(angle_rad)[None]
        new_real = part_real * turn_real - part_imag * turn_imag
        new_imag = part_real * turn_imag + part_imag * turn_real
        return running + jnp.stack([new_real, new_imag], axis=2)

    spec_parts = lax.fori_loop(
        0,
        samples // block_len,
        accumulate,
        jnp.zeros((win_count * chan_count, tw_count, 2, narrow), jnp.float32),
    )
    bin_power = (
        spec_parts[:, :, 0] * spec_parts[:, :, 0] + spec_parts[:, :, 1] * spec_parts[:, :, 1]
    )
    bin_power = bin_power.reshape(-1, band_share)
    padded = padded_2(bin_power, (("fq", 1),), HW)
    row_ids = lax.broadcasted_iota(jnp.int32, (band_share + 2 * HW, band_share), 0)
    col_ids = lax.broadcasted_iota(jnp.int32, (band_share + 2 * HW, band_share), 1)
    box_matrix = ((row_ids - col_ids >= 0) & (row_ids - col_ids <= 2 * HW)).astype(jnp.float32)
    smooth = jnp.dot(
        padded, box_matrix, precision=lax.Precision.HIGHEST, preferred_element_type=jnp.float32
    ) / (2 * HW + 1)
    white_gain = lax.rsqrt(smooth + eps_power).reshape(-1, tw_count, 1, narrow)
    whitened = (
        (spec_parts * white_gain)
        .astype(jnp.bfloat16)
        .reshape(win_count, chan_count, tw_count, 2 * narrow)
    )
    valid_float = valid.astype(jnp.float32)
    source_ids = src_index.reshape(-1)
    src_total = source_ids.shape[0]
    channels_all = valid.shape[1]
    pick_all = (
        lax.broadcasted_iota(jnp.int32, (channels_all, src_total), 0) == source_ids[None, :]
    ).astype(jnp.float32)
    source_valid = jnp.dot(
        valid_float, pick_all, precision=lax.Precision.HIGHEST, preferred_element_type=jnp.float32
    )
    receiver_valid = lax.dynamic_slice_in_dim(valid_float, rx_pos * chan_count, chan_count, 1)
    pair_count = jnp.dot(
        source_valid.T,
        receiver_valid,
        precision=lax.Precision.HIGHEST,
        preferred_element_type=jnp.float32,
    )
    pair_floor = jnp.maximum(pair_count, 1.0)[:, :, None]
    pick_local = (
        source_ids[:, None]
        == rx_pos * chan_count + lax.broadcasted_iota(jnp.int32, (1, chan_count), 1)
    ).astype(jnp.bfloat16)
    inv_scale = 1.0 / math.sqrt(BAND)
    own_block = tw_pos * fq_count + fq_pos
    src_local = src_total // (tw_count * fq_count)
    local_terms = jnp.einsum(
        "sc,wcx->swx",
        pick_local,
        whitened.reshape(win_count, chan_count, tw_count * 2 * narrow),
        preferred_element_type=jnp.float32,
    )
    sources = lax.psum(local_terms.astype(jnp.bfloat16), "rx")
    own_sources = lax.all_to_all(
        sources[None], ("tw", "fq"), split_axis=1, concat_axis=0, tiled=True
    )
    all_windows = lax.all_gather(whitened[None], ("tw", "fq"), axis=0, tiled=True)
    src_valid_own = lax.dynamic_slice_in_dim(source_valid, own_block * src_local, src_local, 1)
    src_valid_own = jnp.transpose(src_valid_own.reshape(tw_count, win_count, src_local), (0, 2, 1))
    own_sources = own_sources.reshape(
        tw_count, fq_count, src_local, win_count, tw_count, 2, narrow
    ) * src_valid_own.reshape(tw_count, 1, src_local, win_count, 1, 1, 1).astype(jnp.bfloat16)
    all_windows = all_windows.reshape(
        tw_count, fq_count, win_count, chan_count, tw_count, 2, narrow
    ) * receiver_valid.reshape(tw_count, 1, win_count, chan_count, 1, 1, 1).astype(jnp.bfloat16)
    src_real = own_sources[..., 0, :]
    src_imag = own_sources[..., 1, :]
    rec_real = all_windows[..., 0, :]
    rec_imag = all_windows[..., 1, :]
    pattern = "tfswbx,tfwcbx->scfbx"
    cross_real = jnp.einsum(
        pattern, src_real, rec_real, preferred_element_type=jnp.float32
    ) + jnp.einsum(pattern, src_imag, rec_imag, preferred_element_type=jnp.float32)
    cross_imag = jnp.einsum(
        pattern, src_real, rec_imag, preferred_element_type=jnp.float32
    ) - jnp.einsum(pattern, src_imag, rec_real, preferred_element_type=jnp.float32)
    floor_own = lax.dynamic_slice_in_dim(pair_floor, own_block * src_local, src_local, 0)
    stacked = jnp.concatenate(
        [
            cross_real.reshape(src_local, chan_count, BAND),
            cross_imag.reshape(src_local, chan_count, BAND),
        ],
        axis=2,
    )
    stacked = (stacked / floor_own).astype(jnp.bfloat16)
    inv_table = inverse_rows(F0 + lax.broadcasted_iota(jnp.int32, (BAND,), 0), LAGS, NT)
    summed = jnp.dot(
        stacked.reshape(src_local * chan_count, 2 * BAND),
        inv_table,
        preferred_element_type=jnp.float32,
    ).reshape(src_local, chan_count, LAGS)
    return (summed * inv_scale).astype(jnp.bfloat16)


def solution(mesh):
    return jax.shard_map(
        shards,
        mesh=mesh,
        in_specs=(P("tw", ("grp", "rx"), None), P("grp", None), P(None, "grp")),
        out_specs=P(("tw", "fq"), ("grp", "rx"), None),
        check_vma=False,
    )
```

profile of v0, /device:TPU:0, one launch (start us, length us, event | category | flops | bytes accessed | tf_op | source)
XLA Modules:
  0.0 195.9 jit_solution(17614216192900421187)
XLA Ops:
  6.6 4.6 %cosine_convert_fusion.1 = (bf16[1024,2,1,128]{3,0,2,1:T(8,128)(2,1)S(1)}, bf16[1024,2,1,128]{3,0,2,1:T(8,128)(2,1)S(1)}) fusion(s32[2,128]{1,0:T(2,128)S(1)} %iota_add_fusion.2), kind=kLoop, calls=%fused_computation.47 | loop fusion | flops 3145728 | bytes 1049600 | tf_op jit(solution)/shard_map/convert.2
  12.4 34.7 %while.16 = (s32[]{:T(128)}, f32[128,2,2,128]{3,2,1,0:T(2,128)S(1)}, bf16[128,15360]{1,0:T(8,128)(2,1)}, bf16[1024,512]{1,0:T(8,128)(2,1)S(1)}, s32[2]{0:T(128)S...) while((s32[]{:T(128)}, f32[128,2,2,128]{3,2,1,0:T(2,128)S(1)}, ...), condition=%wide.region_1.2_spmd.clone, body=%wide.region_0.1_spmd.clone.sunk | while | flops 134613760 | bytes 3412133 | solution.py:78
  12.4 1.3 fusion.68
  14.7 1.3 fusion.68
  17.1 1.3 fusion.68
  21.7 1.3 fusion.68
  26.3 1.3 fusion.68
  31.0 1.3 fusion.68
  35.6 1.3 fusion.68
  40.2 1.3 fusion.68
  44.8 1.3 fusion.68
  47.8 2.4 %collective-permute-start = (f32[128,32]{1,0:T(8,128)S(1)}, f32[128,32]{1,0:T(8,128)S(1)}, u32[]{:S(2)}, u32[]{:S(2)}) collective-permute-start(f32[128,32]{1,0:T(8,128)S(1)} %get-tuple-element.179), channel_id=1, source_target_pairs={{0,1},{2,3},{4,5},{6,7},{8,9},{10,11},{12,13},{14,15},{16,17},{18,... | collective-permute-start | bytes 49160 | tf_op jit(solution)/shard_map/ppermute | solution.py:21
  50.2 1.3 collective-permute-start.1
  51.6 1.7 collective-permute-done.1
  54.0 1.5 fusion.14
  56.1 53.5 %all-reduce.2.cloned.1.call-done = bf16[1,256,4,512]{3,1,2,0:T(8,128)(2,1)} async-done(((bf16[1,256,4,512]{3,1,2,0:T(8,128)(2,1)}), bf16[1,256,4,512]{3,1,2,0:T(8,128)(2,1)}) %all-reduce.2.cloned.1.call-update) | async-done | bytes 1048592 | tf_op jit(solution)/shard_map/psum | solution.py:132
  109.7 3.0 %copy.40 = bf16[1,256,4,512]{3,2,0,1:T(4,128)(2,1)} copy(bf16[1,256,4,512]{3,1,2,0:T(8,128)(2,1)} %all-reduce.2.cloned.1.call-done) | data formatting | bytes 2097152 | tf_op jit(solution)/shard_map/psum | solution.py:132
  112.7 4.3 %all-to-all-start = ((bf16[1,256,4,512]{3,2,0,1:T(4,128)(2,1)}), bf16[1,256,4,512]{3,2,0,1:T(4,128)(2,1)}, u32[]{:S(2)}, u32[]{:S(2)}) async-start(bf16[1,256,4,512]{3,2,0,1:T(4,128)(2,1)} %copy.40), calls=%async_computation | async-start | bytes 2097152 | tf_op jit(solution)/shard_map/all_to_all | solution.py:133
  117.1 5.7 %cosine_convert_fusion = (bf16[512,512]{1,0:T(8,128)(2,1)}, bf16[512,512]{1,0:T(8,128)(2,1)}) fusion(s32[512]{0:T(512)S(1)} %get-tuple-element.185, s32[512]{0:T(512)S(1)} %get-tuple-element.186), kind=kLoop, calls=%fused_computation.40 | loop fusion | flops 3145728 | bytes 1052672 | tf_op jit(solution)/shard_map/convert
  123.0 12.0 %all_gather.3 = bf16[4,4,32,2,256]{4,2,3,1,0:T(8,128)(2,1)S(1)} all-gather(bf16[1,4,32,2,256]{4,2,3,1,0:T(8,128)(2,1)S(1)} %copy.38), channel_id=1, replica_groups=mesh['grp'=2,'rx'=4,'tw'=2,'fq'=2] {'tw','fq'}, dimensions={0}, use_global_device_ids=true | all-gather | bytes 655360 | tf_op jit(solution)/shard_map/all_gather | solution.py:136
  135.1 2.5 %copy.39 = bf16[2,2,4,32,2,2,128]{3,2,0,6,4,1,5:T(4,128)(2,1)} copy(bf16[2,2,4,32,2,2,128]{6,5,3,4,2,1,0:T(2,128)(2,1)S(1)} %reshape.161) | data formatting | bytes 1048576 | tf_op jit(solution)/shard_map/reshape | solution.py:142
  137.7 1.7 broadcast_multiply_fusion.1
  139.4 1.5 reshape.171
  140.9 4.3 %copy.42 = bf16[2,2,64,4,2,2,128]{2,3,0,6,4,1,5:T(4,128)(2,1)} copy(bf16[2,2,64,4,2,2,128]{6,5,4,3,2,1,0:T(2,128)(2,1)S(1)} %reshape.171) | data formatting | bytes 2097152 | tf_op jit(solution)/shard_map/reshape | solution.py:139
  145.1 1.7 broadcast_multiply_fusion
  146.9 1.8 fusion.29
  148.7 4.2 %fusion.30 = f32[2,2,128,32,64,1]{4,3,5,2,1,0:T(8,128)} fusion(bf16[2,2,64,4,2,2,128]{2,3,0,6,4,1,5:T(4,128)(2,1)S(1)} %bitcast.78, bf16[2,2,4,32,2,2,128]{3,2,0,6,4,1,5:T(4,128)(2,1)S(1)} %bitcast.74), kind=kOutput, calls=%fused_computation.54 | convolution fusion | flops 16777216 | bytes 6291456 | tf_op jit(solution)/shard_map/tfswbx,tfwcbx->scfbx/dot_general | solution.py:153
  152.9 4.3 %bitcast_add_fusion = f32[2,2,128,32,64]{4,3,2,1,0:T(8,128)} fusion(f32[2,2,128,32,64,1]{4,3,5,2,1,0:T(8,128)S(1)} %fusion.29, bf16[2,2,4,32,2,2,128]{3,2,0,6,4,1,5:T(4,128)(2,1)S(1)} %bitcast.75, bf16[2,2,64,4,2,2,128]{2,3,0,6,4,1,5:T(4,128)(2,1)S(1)} %bitcast.79), kind=kOutput, calls=%fused_computation.17 | convolution fusion | flops 17825792 | bytes 14680064 | tf_op jit(solution)/shard_map/tfswbx,tfwcbx->scfbx/dot_general | solution.py:152
  157.2 7.7 %copy.43 = f32[64,32,512]{2,1,0:T(8,128)} copy(f32[64,32,512]{0,1,2:T(8,128)} %bitcast.72) | data formatting | bytes 8388608 | tf_op jit(solution)/shard_map/concatenate | solution.py:157
  165.0 9.1 %bitcast_subtract_fusion = f32[2,2,128,32,64]{4,3,2,1,0:T(8,128)} fusion(f32[2,2,128,32,64,1]{4,3,5,2,1,0:T(8,128)} %fusion.30, bf16[2,2,4,32,2,2,128]{3,2,0,6,4,1,5:T(4,128)(2,1)S(1)} %bitcast.76, bf16[2,2,64,4,2,2,128]{2,3,0,6,4,1,5:T(4,128)(2,1)} %bitcast.80), kind=kOutput, calls=%fused_computation.16 | convolution fusion | flops 17825792 | bytes 14680064 | tf_op jit(solution)/shard_map/tfswbx,tfwcbx->scfbx/dot_general | solution.py:155
  174.0 7.8 %copy.44 = f32[64,32,512]{2,1,0:T(8,128)} copy(f32[64,32,512]{0,1,2:T(8,128)} %bitcast.71) | data formatting | bytes 8388608 | tf_op jit(solution)/shard_map/concatenate | solution.py:157
  181.8 7.2 %multiply_convert_fusion = bf16[64,32,512]{2,1,0:T(8,128)(2,1)} fusion(f32[64,32,512]{2,1,0:T(8,128)} %copy.44, f32[64,32,512]{2,1,0:T(8,128)} %copy.43, f32[64,32]{1,0:T(8,128)S(1)} %copy.45, bf16[512,512]{1,0:T(8,128)(2,1)S(1)} %copy-done.2, bf16[512,512]{1,0:T(8,128)(2,1)S(1)} %copy-done.1), kind=kOutput, calls=%fused_computation.18 | convolution fusion | flops 2157969408 | bytes 11542528 | tf_op jit(solution)/shard_map/dot_general | solution.py:166
  (106 shorter events, 26.4 us)
Async XLA Ops:
  6.5 103.1 %all-reduce.2.cloned.1.call-start = ((), (), s32[]{:S(2)}) async-start(), calls=%async_computation.1 | async-start | bytes 2097152 | tf_op jit(solution)/shard_map/psum | solution.py:132
  12.4 39.1 %copy-start.4 = (s32[4,64]{1,0:T(4,128)S(1)}, s32[4,64]{1,0:T(4,128)}, u32[]{:S(2)}) copy-start(s32[4,64]{1,0:T(4,128)} %param.6) | copy-start | bytes 3076
  47.7 7.8 %copy-start.3 = (s32[8,128]{1,0:T(8,128)S(1)}, s32[8,128]{1,0:T(8,128)}, u32[]{:S(2)}) copy-start(s32[8,128]{1,0:T(8,128)} %param.7) | copy-start | bytes 12292
  47.8 3.8 %collective-permute-start = (f32[128,32]{1,0:T(8,128)S(1)}, f32[128,32]{1,0:T(8,128)S(1)}, u32[]{:S(2)}, u32[]{:S(2)}) collective-permute-start(f32[128,32]{1,0:T(8,128)S(1)} %get-tuple-element.179), channel_id=1, source_target_pairs={{0,1},{2,3},{4,5},{6,7},{8,9},{10,11},{12,13},{14,15},{16,17},{18,... | collective-permute-start | bytes 49160 | tf_op jit(solution)/shard_map/ppermute | solution.py:21
  50.2 3.1 %collective-permute-start.1 = (f32[128,32]{1,0:T(8,128)S(1)}, f32[128,32]{1,0:T(8,128)S(1)}, u32[]{:S(2)}, u32[]{:S(2)}) collective-permute-start(f32[128,32]{1,0:T(8,128)S(1)} %get-tuple-element.180), channel_id=1, source_target_pairs={{1,0},{3,2},{5,4},{7,6},{9,8},{11,10},{13,12},{15,14},{17,16},{19,... | collective-permute-start | bytes 49160 | tf_op jit(solution)/shard_map/ppermute | solution.py:24
  112.7 26.7 %all-to-all-start = ((bf16[1,256,4,512]{3,2,0,1:T(4,128)(2,1)}), bf16[1,256,4,512]{3,2,0,1:T(4,128)(2,1)}, u32[]{:S(2)}, u32[]{:S(2)}) async-start(bf16[1,256,4,512]{3,2,0,1:T(4,128)(2,1)} %copy.40), calls=%async_computation | async-start | bytes 2097152 | tf_op jit(solution)/shard_map/all_to_all | solution.py:133
  146.9 6.0 %copy-start = (bf16[1,2,64,8,2,2,128]{2,3,0,6,4,1,5:T(8,128)(2,1)}, bf16[1,2,64,8,2,2,128]{2,3,0,6,4,1,5:T(8,128)(2,1)S(1)}, u32[]{:S(2)}) copy-start(bf16[1,2,64,8,2,2,128]{2,3,0,6,4,1,5:T(8,128)(2,1)S(1)} %broadcast_multiply_fusion) | copy-start | bytes 3145732
  174.0 7.8 %copy-start.1 = (bf16[512,512]{1,0:T(8,128)(2,1)S(1)}, bf16[512,512]{1,0:T(8,128)(2,1)}, u32[]{:S(2)}) copy-start(bf16[512,512]{1,0:T(8,128)(2,1)} %get-tuple-element.181) | copy-start | bytes 1572868
  174.0 7.8 %copy-start.2 = (bf16[512,512]{1,0:T(8,128)(2,1)S(1)}, bf16[512,512]{1,0:T(8,128)(2,1)}, u32[]{:S(2)}) copy-start(bf16[512,512]{1,0:T(8,128)(2,1)} %get-tuple-element.182) | copy-start | bytes 1572868
Sparse Core Ops, SparseCore 0:
  55.6 54.0 all-reduce.1
where the time goes:
time: 197 us; the launch traced here: 196 us
  waiting for transfers between devices  55.3 us (28%)
  matrix products  47.8 us (24%)
  local copies, waits for them, and re-layouts  31.2 us (16%)
  other arithmetic  27.4 us (14%)
  between operations  13.6 us (7%)
  blocking collectives  12 us (6%)
  starting transfers between devices  7.95 us (4%)
    psum x1, waiting for transfers between devices, shards(): sources = lax.psum(local_terms.astype(jnp.bfloat16), 'rx')  53.5 us
    dot_general x15, matrix products, accumulate(): jnp.dot(trace_piece, base_table, preferred_element_type=jnp.float32)  18.9 us
    concatenate x2, local copies, waits for them, and re-layouts, shards(): jnp.concatenate([cross_real.reshape(src_local, chan_count, BAND), cross_i...  15.5 us
    all_gather x1, blocking collectives, shards(): lax.all_gather(whitened[None], ('tw', 'fq'), axis=0, tiled=True)  12 us
    another operation x2, other arithmetic  10.3 us
    dot_general x1, matrix products, shards(): jnp.einsum(pattern, src_imag, rec_real, preferred_element_type=jnp.float32)  9.08 us
    dot_general x1, matrix products, shards(): jnp.dot(stacked.reshape(src_local * chan_count, 2 * BAND), inv_table, pre...  7.22 us
    add x15, other arithmetic, accumulate(): return running + jnp.stack([new_real, new_imag], axis=2)  6.72 us
  transfers between devices with their start and end apart: 4, of which 2 were waited for; matrix products, arithmetic and copies ran while one was open for 6% of the time, Pallas kernels for 0%

commit v1 on v0

--- a/solution.py
+++ b/solution.py
@@ -1,3 +1,4 @@
+import functools
 import math
 import jax
 import jax.numpy as jnp
@@ -11,6 +12,19 @@
 LAGS = 512
 two_pi = 2.0 * math.pi
 eps_power = 1e-05
+
+
+def lay_matrix_for(panel, join_dim):
+    lower = jnp.concatenate(
+        jax.lax.all_to_all(
+            jnp.stack(jax.lax.axis_size(("tw", "fq")) * [panel], axis=0), ("tw", "fq"), 0, 0
+        ),
+        axis=join_dim,
+    )
+    return lower
+
+
+enter_the_frame = functools.partial(lay_matrix_for, join_dim=0)
 
 
 def padded_2(block, sides, width):
@@ -133,7 +147,7 @@
     own_sources = lax.all_to_all(
         sources[None], ("tw", "fq"), split_axis=1, concat_axis=0, tiled=True
     )
-    all_windows = lax.all_gather(whitened[None], ("tw", "fq"), axis=0, tiled=True)
+    all_windows = enter_the_frame(whitened[None])
     src_valid_own = lax.dynamic_slice_in_dim(source_valid, own_block * src_local, src_local, 1)
     src_valid_own = jnp.transpose(src_valid_own.reshape(tw_count, win_count, src_local), (0, 2, 1))
     own_sources = own_sources.reshape(

time: 197 us -> 189 us (0.959)
  blocking collectives: 12 us -> 0 us
  starting transfers between devices: 7.95 us -> 11.7 us
    all_gather x1 -> x0, blocking collectives: 12 us -> none  [shards(): lax.all_gather(whitened[None], ('tw', 'fq'), axis=0, tiled=True)]
    psum x1, waiting for transfers between devices: 53.5 us -> 48.8 us  [shards(): sources = lax.psum(local_terms.astype(jnp.bfloat16), 'rx')]
    all_to_all x1, waiting for transfers between devices: 0.01 us -> 4.12 us  [shards(): lax.all_to_all(sources[None], ('tw', 'fq'), split_axis=1, concat_axis=0,...]
    all_to_all x0 -> x1, starting transfers between devices: none -> 3.6 us  [lay_matrix_for(): jax.lax.all_to_all(jnp.stack(jax.lax.axis_size(('tw', 'fq')) * [panel], a...]
    another operation x3 -> x6, local copies, waits for them, and re-layouts: 0.18 us -> 3.74 us  [the longest x2 2.66 us: shards(): all_windows.reshape(tw_count, fq_count, win_count, chan_count, tw_count,...]
    reshape x2 -> x0, local copies, waits for them, and re-layouts: 2.66 us -> none  [shards(): all_windows.reshape(tw_count, fq_count, win_count, chan_count, tw_count,...]
  transfers between devices with their start and end apart: 4 -> 5, of which waited for: 2 -> 3; matrix products, arithmetic and copies ran while one was open for 6% -> 8% of each run, Pallas kernels for 0% -> 0%
where the time goes in v1:
time: 189 us; the launch traced here: 188 us
  waiting for transfers between devices  54.7 us (29%)
  matrix products  47.7 us (25%)
  local copies, waits for them, and re-layouts  32 us (17%)
  other arithmetic  27.4 us (14%)
  between operations  13.6 us (7%)
  starting transfers between devices  11.7 us (6%)
    psum x1, waiting for transfers between devices, shards(): sources = lax.psum(local_terms.astype(jnp.bfloat16), 'rx')  48.8 us
    dot_general x15, matrix products, accumulate(): jnp.dot(trace_piece, base_table, preferred_element_type=jnp.float32)  18.9 us
    concatenate x2, local copies, waits for them, and re-layouts, shards(): jnp.concatenate([cross_real.reshape(src_local, chan_count, BAND), cross_i...  15.4 us
    another operation x2, other arithmetic  10.3 us
    dot_general x1, matrix products, shards(): jnp.einsum(pattern, src_imag, rec_real, preferred_element_type=jnp.float32)  9.07 us
    dot_general x1, matrix products, shards(): jnp.dot(stacked.reshape(src_local * chan_count, 2 * BAND), inv_table, pre...  7.22 us
    add x15, other arithmetic, accumulate(): return running + jnp.stack([new_real, new_imag], axis=2)  6.72 us
    reshape x2, local copies, waits for them, and re-layouts, shards(): own_sources.reshape(tw_count, fq_count, src_local, win_count, tw_count, 2...  5.72 us
  transfers between devices with their start and end apart: 5, of which 3 were waited for; matrix products, arithmetic and copies ran while one was open for 8% of the time, Pallas kernels for 0%

profile of v1, /device:TPU:0, one launch (start us, length us, event | category | flops | bytes accessed | tf_op | source)
XLA Modules:
  0.0 187.8 jit_solution(7708293239737642877)
XLA Ops:
  6.6 4.6 %cosine_convert_fusion.1 = (bf16[1024,2,1,128]{3,0,2,1:T(8,128)(2,1)S(1)}, bf16[1024,2,1,128]{3,0,2,1:T(8,128)(2,1)S(1)}) fusion(s32[2,128]{1,0:T(2,128)S(1)} %iota_add_fusion.2), kind=kLoop, calls=%fused_computation.47 | loop fusion | flops 3145728 | bytes 1049600 | tf_op jit(solution)/shard_map/convert.2
  12.4 34.7 %while.16 = (s32[]{:T(128)}, f32[128,2,2,128]{3,2,1,0:T(2,128)S(1)}, bf16[128,15360]{1,0:T(8,128)(2,1)}, bf16[1024,512]{1,0:T(8,128)(2,1)S(1)}, s32[2]{0:T(128)S...) while((s32[]{:T(128)}, f32[128,2,2,128]{3,2,1,0:T(2,128)S(1)}, ...), condition=%wide.region_1.2_spmd.clone, body=%wide.region_0.1_spmd.clone.sunk | while | flops 134613760 | bytes 3412133 | solution.py:92
  12.4 1.3 fusion.68
  14.7 1.3 fusion.68
  21.7 1.3 fusion.68
  26.3 1.3 fusion.68
  31.0 1.3 fusion.68
  35.6 1.3 fusion.68
  40.2 1.3 fusion.68
  44.8 1.3 fusion.68
  47.8 2.4 %collective-permute-start = (f32[128,32]{1,0:T(8,128)S(1)}, f32[128,32]{1,0:T(8,128)S(1)}, u32[]{:S(2)}, u32[]{:S(2)}) collective-permute-start(f32[128,32]{1,0:T(8,128)S(1)} %get-tuple-element.179), channel_id=1, source_target_pairs={{0,1},{2,3},{4,5},{6,7},{8,9},{10,11},{12,13},{14,15},{16,17},{18,... | collective-permute-start | bytes 49160 | tf_op jit(solution)/shard_map/ppermute | solution.py:35
  50.2 1.3 collective-permute-start.1
  51.6 1.7 collective-permute-done.1
  54.0 1.5 fusion.14
  56.7 3.6 %all-to-all-start = ((bf16[4,1,4,32,2,256]{5,3,4,2,1,0:T(8,128)(2,1)}), bf16[4,1,4,32,2,256]{5,3,4,2,1,0:T(8,128)(2,1)S(1)}, u32[]{:S(2)}, u32[]{:S(2)}) async-start(bf16[4,1,4,32,2,256]{5,3,4,2,1,0:T(8,128)(2,1)} %stack.26), calls=%async_computation | async-start | bytes 1048576 | tf_op jit(solution)/shard_map/all_to_all | solution.py:19
  60.8 48.8 %all-reduce.2.cloned.1.call-done = bf16[1,256,4,512]{3,1,2,0:T(8,128)(2,1)} async-done(((bf16[1,256,4,512]{3,1,2,0:T(8,128)(2,1)}), bf16[1,256,4,512]{3,1,2,0:T(8,128)(2,1)}) %all-reduce.2.cloned.1.call-update) | async-done | bytes 1048592 | tf_op jit(solution)/shard_map/psum | solution.py:146
  109.6 3.0 %copy.38 = bf16[1,256,4,512]{3,2,0,1:T(4,128)(2,1)} copy(bf16[1,256,4,512]{3,1,2,0:T(8,128)(2,1)} %all-reduce.2.cloned.1.call-done) | data formatting | bytes 2097152 | tf_op jit(solution)/shard_map/psum | solution.py:146
  112.6 4.4 %all-to-all-start.1 = ((bf16[1,256,4,512]{3,2,0,1:T(4,128)(2,1)}), bf16[1,256,4,512]{3,2,0,1:T(4,128)(2,1)}, u32[]{:S(2)}, u32[]{:S(2)}) async-start(bf16[1,256,4,512]{3,2,0,1:T(4,128)(2,1)} %copy.38), calls=%async_computation.1 | async-start | bytes 2097152 | tf_op jit(solution)/shard_map/all_to_all | solution.py:147
  117.2 5.7 %cosine_convert_fusion = (bf16[512,512]{1,0:T(8,128)(2,1)}, bf16[512,512]{1,0:T(8,128)(2,1)}) fusion(s32[512]{0:T(512)S(1)} %get-tuple-element.185, s32[512]{0:T(512)S(1)} %get-tuple-element.186), kind=kLoop, calls=%fused_computation.40 | loop fusion | flops 3145728 | bytes 1052672 | tf_op jit(solution)/shard_map/convert
  123.0 2.5 %copy.37 = bf16[2,2,4,32,2,2,128]{3,2,0,6,4,1,5:T(4,128)(2,1)} copy(bf16[2,2,4,32,2,2,128]{6,5,3,4,2,1,0:T(2,128)(2,1)S(1)} %reshape_reshape.6) | data formatting | bytes 1048576 | tf_op jit(solution)/shard_map/reshape;reshape | solution.py:156
  125.5 1.7 broadcast_multiply_fusion.1
  127.3 4.1 %all-to-all-done.1 = bf16[1,256,4,512]{3,2,0,1:T(4,128)(2,1)} async-done(((bf16[1,256,4,512]{3,2,0,1:T(4,128)(2,1)}), bf16[1,256,4,512]{3,2,0,1:T(4,128)(2,1)}, u32[]{:S(2)}, u32[]{:S(2)}) %all-to-all-start.1) | async-done | bytes 1048608 | tf_op jit(solution)/shard_map/all_to_all | solution.py:147
  131.4 1.5 reshape.170
  132.9 4.3 %copy.40 = bf16[2,2,64,4,2,2,128]{2,3,0,6,4,1,5:T(4,128)(2,1)} copy(bf16[2,2,64,4,2,2,128]{6,5,4,3,2,1,0:T(2,128)(2,1)S(1)} %reshape.170) | data formatting | bytes 2097152 | tf_op jit(solution)/shard_map/reshape | solution.py:153
  137.1 1.7 broadcast_multiply_fusion
  138.9 1.8 fusion.29
  140.6 4.2 %fusion.30 = f32[2,2,128,32,64,1]{4,3,5,2,1,0:T(8,128)} fusion(bf16[2,2,64,4,2,2,128]{2,3,0,6,4,1,5:T(4,128)(2,1)S(1)} %bitcast.78, bf16[2,2,4,32,2,2,128]{3,2,0,6,4,1,5:T(4,128)(2,1)S(1)} %bitcast.74), kind=kOutput, calls=%fused_computation.54 | convolution fusion | flops 16777216 | bytes 6291456 | tf_op jit(solution)/shard_map/tfswbx,tfwcbx->scfbx/dot_general | solution.py:167
  144.8 4.4 %bitcast_add_fusion = f32[2,2,128,32,64]{4,3,2,1,0:T(8,128)} fusion(f32[2,2,128,32,64,1]{4,3,5,2,1,0:T(8,128)S(1)} %fusion.29, bf16[2,2,4,32,2,2,128]{3,2,0,6,4,1,5:T(4,128)(2,1)S(1)} %bitcast.75, bf16[2,2,64,4,2,2,128]{2,3,0,6,4,1,5:T(4,128)(2,1)S(1)} %bitcast.79), kind=kOutput, calls=%fused_computation.17 | convolution fusion | flops 17825792 | bytes 14680064 | tf_op jit(solution)/shard_map/tfswbx,tfwcbx->scfbx/dot_general | solution.py:166
  149.2 7.7 %copy.41 = f32[64,32,512]{2,1,0:T(8,128)} copy(f32[64,32,512]{0,1,2:T(8,128)} %bitcast.72) | data formatting | bytes 8388608 | tf_op jit(solution)/shard_map/concatenate | solution.py:171
  156.8 9.1 %bitcast_subtract_fusion = f32[2,2,128,32,64]{4,3,2,1,0:T(8,128)} fusion(f32[2,2,128,32,64,1]{4,3,5,2,1,0:T(8,128)} %fusion.30, bf16[2,2,4,32,2,2,128]{3,2,0,6,4,1,5:T(4,128)(2,1)S(1)} %bitcast.76, bf16[2,2,64,4,2,2,128]{2,3,0,6,4,1,5:T(4,128)(2,1)} %bitcast.80), kind=kOutput, calls=%fused_computation.16 | convolution fusion | flops 17825792 | bytes 14680064 | tf_op jit(solution)/shard_map/tfswbx,tfwcbx->scfbx/dot_general | solution.py:169
  165.9 7.8 %copy.42 = f32[64,32,512]{2,1,0:T(8,128)} copy(f32[64,32,512]{0,1,2:T(8,128)} %bitcast.71) | data formatting | bytes 8388608 | tf_op jit(solution)/shard_map/concatenate | solution.py:171
  173.7 7.2 %multiply_convert_fusion = bf16[64,32,512]{2,1,0:T(8,128)(2,1)} fusion(f32[64,32,512]{2,1,0:T(8,128)} %copy.42, f32[64,32,512]{2,1,0:T(8,128)} %copy.41, f32[64,32]{1,0:T(8,128)S(1)} %copy.43, bf16[512,512]{1,0:T(8,128)(2,1)S(1)} %copy-done.2, bf16[512,512]{1,0:T(8,128)(2,1)S(1)} %copy-done.1), kind=kOutput, calls=%fused_computation.18 | convolution fusion | flops 2157969408 | bytes 11542528 | tf_op jit(solution)/shard_map/dot_general | solution.py:180
  (108 shorter events, 28.5 us)
Async XLA Ops:
  6.5 103.1 %all-reduce.2.cloned.1.call-start = ((), (), s32[]{:S(2)}) async-start(), calls=%async_computation.2 | async-start | bytes 2097152 | tf_op jit(solution)/shard_map/psum | solution.py:146
  12.4 39.1 %copy-start.4 = (s32[4,64]{1,0:T(4,128)S(1)}, s32[4,64]{1,0:T(4,128)}, u32[]{:S(2)}) copy-start(s32[4,64]{1,0:T(4,128)} %param.6) | copy-start | bytes 3076
  47.7 7.8 %copy-start.3 = (s32[8,128]{1,0:T(8,128)S(1)}, s32[8,128]{1,0:T(8,128)}, u32[]{:S(2)}) copy-start(s32[8,128]{1,0:T(8,128)} %param.7) | copy-start | bytes 12292
  47.8 3.8 %collective-permute-start = (f32[128,32]{1,0:T(8,128)S(1)}, f32[128,32]{1,0:T(8,128)S(1)}, u32[]{:S(2)}, u32[]{:S(2)}) collective-permute-start(f32[128,32]{1,0:T(8,128)S(1)} %get-tuple-element.179), channel_id=1, source_target_pairs={{0,1},{2,3},{4,5},{6,7},{8,9},{10,11},{12,13},{14,15},{16,17},{18,... | collective-permute-start | bytes 49160 | tf_op jit(solution)/shard_map/ppermute | solution.py:35
  50.2 3.1 %collective-permute-start.1 = (f32[128,32]{1,0:T(8,128)S(1)}, f32[128,32]{1,0:T(8,128)S(1)}, u32[]{:S(2)}, u32[]{:S(2)}) collective-permute-start(f32[128,32]{1,0:T(8,128)S(1)} %get-tuple-element.180), channel_id=1, source_target_pairs={{1,0},{3,2},{5,4},{7,6},{9,8},{11,10},{13,12},{15,14},{17,16},{19,... | collective-permute-start | bytes 49160 | tf_op jit(solution)/shard_map/ppermute | solution.py:38
  56.7 56.0 %all-to-all-start = ((bf16[4,1,4,32,2,256]{5,3,4,2,1,0:T(8,128)(2,1)}), bf16[4,1,4,32,2,256]{5,3,4,2,1,0:T(8,128)(2,1)S(1)}, u32[]{:S(2)}, u32[]{:S(2)}) async-start(bf16[4,1,4,32,2,256]{5,3,4,2,1,0:T(8,128)(2,1)} %stack.26), calls=%async_computation | async-start | bytes 1048576 | tf_op jit(solution)/shard_map/all_to_all | solution.py:19
  112.6 18.8 %all-to-all-start.1 = ((bf16[1,256,4,512]{3,2,0,1:T(4,128)(2,1)}), bf16[1,256,4,512]{3,2,0,1:T(4,128)(2,1)}, u32[]{:S(2)}, u32[]{:S(2)}) async-start(bf16[1,256,4,512]{3,2,0,1:T(4,128)(2,1)} %copy.38), calls=%async_computation.1 | async-start | bytes 2097152 | tf_op jit(solution)/shard_map/all_to_all | solution.py:147
  138.9 6.0 %copy-start = (bf16[1,2,64,8,2,2,128]{2,3,0,6,4,1,5:T(8,128)(2,1)}, bf16[1,2,64,8,2,2,128]{2,3,0,6,4,1,5:T(8,128)(2,1)S(1)}, u32[]{:S(2)}) copy-start(bf16[1,2,64,8,2,2,128]{2,3,0,6,4,1,5:T(8,128)(2,1)S(1)} %broadcast_multiply_fusion) | copy-start | bytes 3145732
  165.9 7.8 %copy-start.1 = (bf16[512,512]{1,0:T(8,128)(2,1)S(1)}, bf16[512,512]{1,0:T(8,128)(2,1)}, u32[]{:S(2)}) copy-start(bf16[512,512]{1,0:T(8,128)(2,1)} %get-tuple-element.181) | copy-start | bytes 1572868
  165.9 7.8 %copy-start.2 = (bf16[512,512]{1,0:T(8,128)(2,1)S(1)}, bf16[512,512]{1,0:T(8,128)(2,1)}, u32[]{:S(2)}) copy-start(bf16[512,512]{1,0:T(8,128)(2,1)} %get-tuple-element.182) | copy-start | bytes 1572868
Sparse Core Ops, SparseCore 0:
  55.6 53.9 all-reduce.1
